TPU v7x, 32 devices: a whole 2x2x4 slice. The times are simulated.
32 devices in a mesh: blade: 1, prow: 4 (over x, core), pcol: 8 (over z, y).
Axes of the slice: x: 2, y: 2, z: 4, core: 2. Of those that a mesh axis runs over, the one named last changes fastest.
Arguments:
- factor: float32 [4, 4, 512, 4, 8, 256], P('blade', 'prow', None, None, 'pcol'), may hold values from -0.03125 to 0.03125
- inverses: float32 [4, 8, 256, 4, 512], P('blade', 'pcol', None, 'prow'), as said below
- targets: float32 [8, 3, 8192], P('blade'), may hold values from -6 to 6
- anchors: float32 [3, 8192], P('blade'), may hold values from 0 to 1, as said below
- nodes: float32 [3, 16, 128, 128], P('blade', 'prow', 'pcol'), as said below
Outputs:
- coefficients: float32 [8, 3, 8192], P('blade')
- moved: float32 [8, 3, 16, 128, 128], P('blade', None, 'prow', 'pcol')
- jacobian: float32 [8, 16, 128, 128], P('blade', 'prow', 'pcol')
Inputs may be any that keep to these rules, and one draw needn't show every extreme that they name: `inverses`: 4 blocks of 2048 x 2048 real entries. `anchors`: positions in the unit cube. `nodes`: positions inside a box around the unit cube, ordered along span, chord and normal.
All inputs are finite; a program needn't handle non-finite values.
Results may differ from a plain program's by a relative error of at most 0.0003.
Values sent between devices are 32-bit elements; how exact they have to be, the bound alone decides.
A program may use at most 64 MiB of HBM per device.

v0:
```python
import math
import jax
import jax.numpy as jnp
from jax import lax
from jax.sharding import PartitionSpec as P

support_radius = 0.1
highest = lax.Precision.HIGHEST


def padded_2(cells, sides, width):
    for axis, dim in sides:
        count = lax.axis_size(axis)
        ends = count - 1
        head = lax.slice_in_dim(cells, 0, width, axis=dim)
        tail = lax.slice_in_dim(cells, cells.shape[dim] - width, cells.shape[dim], axis=dim)
        cells = jnp.concatenate(
            [
                lax.ppermute(tail, axis, [(i, (i + 1) % count) for i in range(ends)]),
                cells,
                lax.ppermute(head, axis, [((i + 1) % count, i) for i in range(ends)]),
            ],
            axis=dim,
        )
    return cells


def wendland(dist_sq):
    scaled_dist = jnp.sqrt(dist_sq) / support_radius
    falloff = jnp.maximum(1.0 - scaled_dist, 0.0)
    return falloff**4 * (4.0 * scaled_dist + 1.0)


def extend(values, axis_pos):
    extent = values.shape[axis_pos]
    low_layer = 2.0 * lax.slice_in_dim(values, 0, 1, axis=axis_pos) - lax.slice_in_dim(
        values, 1, 2, axis=axis_pos
    )
    high_layer = 2.0 * lax.slice_in_dim(
        values, extent - 1, extent, axis=axis_pos
    ) - lax.slice_in_dim(values, extent - 2, extent - 1, axis=axis_pos)
    return jnp.concatenate([low_layer, values, high_layer], axis=axis_pos)


def close_edges(padded, axis_pos, at_low, at_high):
    extent = padded.shape[axis_pos]
    low_layer = 2.0 * lax.slice_in_dim(padded, 1, 2, axis=axis_pos) - lax.slice_in_dim(
        padded, 2, 3, axis=axis_pos
    )
    high_layer = 2.0 * lax.slice_in_dim(
        padded, extent - 2, extent - 1, axis=axis_pos
    ) - lax.slice_in_dim(padded, extent - 3, extent - 2, axis=axis_pos)
    first_layer = jnp.where(at_low, low_layer, lax.slice_in_dim(padded, 0, 1, axis=axis_pos))
    last_layer = jnp.where(
        at_high, high_layer, lax.slice_in_dim(padded, extent - 1, extent, axis=axis_pos)
    )
    inner_layers = lax.slice_in_dim(padded, 1, extent - 1, axis=axis_pos)
    return jnp.concatenate([first_layer, inner_layers, last_layer], axis=axis_pos)


def jacobian_of(extended, scales):
    d_span = (extended[:, :, 2:, 1:-1, 1:-1] - extended[:, :, :-2, 1:-1, 1:-1]) * scales[0]
    d_chord = (extended[:, :, 1:-1, 2:, 1:-1] - extended[:, :, 1:-1, :-2, 1:-1]) * scales[1]
    d_normal = (extended[:, :, 1:-1, 1:-1, 2:] - extended[:, :, 1:-1, 1:-1, :-2]) * scales[2]
    cross_first = d_chord[:, 1] * d_normal[:, 2] - d_chord[:, 2] * d_normal[:, 1]
    cross_second = d_chord[:, 2] * d_normal[:, 0] - d_chord[:, 0] * d_normal[:, 2]
    cross_third = d_chord[:, 0] * d_normal[:, 1] - d_chord[:, 1] * d_normal[:, 0]
    return d_span[:, 0] * cross_first + d_span[:, 1] * cross_second + d_span[:, 2] * cross_third


def shards(factor, inverses, targets, anchors, nodes):
    row_devs = lax.axis_size("prow")
    col_devs = lax.axis_size("pcol")
    prow_id = lax.axis_index("prow")
    pcol_id = lax.axis_index("pcol")
    local_factor = factor[:, 0, :, :, 0, :]
    local_inverses = inverses[:, 0, :, 0, :]
    block_total = local_factor.shape[0]
    row_piece = local_factor.shape[1]
    col_piece = local_factor.shape[3]
    block_len = row_piece * row_devs
    instances = targets.shape[0]
    row_count = instances * targets.shape[1]
    point_total = targets.shape[2]
    right_sides = targets.reshape(row_count, block_total, block_len)
    forward = jnp.zeros((row_count, block_total, col_piece), jnp.float32)
    for block_id in range(block_total):
        partial_value = jnp.einsum(
            "rjc,wjc->wr", local_factor[block_id], forward, precision=highest
        )
        own_rows = lax.dynamic_slice_in_dim(
            right_sides[:, block_id], prow_id * row_piece, row_piece, 1
        )
        summed = lax.psum(partial_value, "pcol")
        term = jnp.einsum(
            "ab,wb->wa", local_inverses[block_id], own_rows - summed, precision=highest
        )
        solved = lax.psum(term, "prow")
        forward = forward.at[:, block_id].set(solved)
    coeffs = jnp.zeros((row_count, block_total, row_piece), jnp.float32)
    for block_id in reversed(range(block_total)):
        col_blocks = local_factor[:, :, block_id]
        forward_block = forward[:, block_id]
        partial_value = jnp.einsum("jrc,wjr->wc", col_blocks, coeffs, precision=highest)
        summed = lax.psum(partial_value, "prow")
        term = jnp.einsum(
            "ab,wa->wb", local_inverses[block_id], forward_block - summed, precision=highest
        )
        solved = lax.psum(term, "pcol")
        coeffs = coeffs.at[:, block_id].set(solved)
    coeffs = lax.all_gather(coeffs, "prow", axis=2, tiled=True)
    coef_matrix = coeffs.reshape(row_count, point_total)
    flat = nodes.reshape(3, -1)
    node_count = flat.shape[1]
    block_size = min(512, node_count)
    node_groups = flat.reshape(3, node_count // block_size, block_size).transpose(1, 0, 2)

    def deform(node_group):
        dist_sq = (node_group[0][:, None] - anchors[0][None, :]) ** 2
        dist_sq = dist_sq + (node_group[1][:, None] - anchors[1][None, :]) ** 2
        dist_sq = dist_sq + (node_group[2][:, None] - anchors[2][None, :]) ** 2
        return lax.dot_general(
            coef_matrix, wendland(dist_sq), (((1,), (1,)), ((), ())), precision=highest
        )

    shifts = lax.map(deform, node_groups)
    shifts = shifts.transpose(1, 0, 2).reshape((instances,) + nodes.shape)
    moved = nodes[None] + 2.0 / math.sqrt(point_total) * shifts
    padded = padded_2(moved, (("prow", 2), ("pcol", 3)), 1)
    padded = close_edges(padded, 2, prow_id == 0, prow_id == row_devs - 1)
    padded = close_edges(padded, 3, pcol_id == 0, pcol_id == col_devs - 1)
    extended = extend(padded, 4)
    scales = (
        nodes.shape[1] * row_devs / 2.0,
        nodes.shape[2] * col_devs / 2.0,
        nodes.shape[3] / 2.0,
    )
    jacobian = jacobian_of(extended, scales)
    return (coeffs.reshape(instances, 3, point_total), moved, jacobian)


def solution(mesh):
    placed = (
        P("blade", "prow", None, None, "pcol", None),
        P("blade", "pcol", None, "prow", None),
        P("blade", None, None),
        P("blade", None),
        P("blade", "prow", "pcol", None),
    )
    return jax.shard_map(
        shards,
        mesh=mesh,
        in_specs=placed,
        out_specs=(
            P("blade", None, None),
            P("blade", None, "prow", "pcol", None),
            P("blade", "prow", "pcol", None),
        ),
        check_vma=False,
    )
```

profile of v0, /device:TPU:1, one launch (start us, length us, event | category | flops | bytes accessed | tf_op | source)
XLA Modules:
  0.0 1282.0 jit_solution(8106645865025207151)
XLA Ops:
  0.6 9.3 fusion.125
  9.9 8.8 copy.127
  20.0 1.2 fusion.129
  21.3 3.9 fusion.126
  25.2 4.6 copy.27
  29.8 1.7 fusion.58
  31.5 32.1 %psum.112 = f32[24,512]{1,0:T(8,128)S(1)} all-reduce(f32[24,512]{1,0:T(8,128)} %fusion.58), channel_id=1, replica_groups=mesh['blade'=1,'prow'=4,'pcol'=8] {'pcol'}, use_global_device_ids=true, to_apply=%region_0.0 | all-reduce | flops 12288 | bytes 98304 | tf_op jit(solution)/shard_map/psum | solution.py:94
  64.9 18.3 %psum.113 = f32[24,1,256]{2,0,1:T(8,128)} all-reduce(f32[24,1,256]{2,0,1:T(8,128)S(1)} %convolution_bitcast_fusion.5), channel_id=1, replica_groups=mesh['blade'=1,'prow'=4,'pcol'=8] {'prow'}, use_global_device_ids=true, to_apply=%region_1.0 | all-reduce | flops 6144 | bytes 49152 | tf_op jit(solution)/shard_map/psum | solution.py:98
  83.2 4.6 copy.28
  87.8 2.5 fusion.61
  90.3 27.0 %psum.114 = f32[24,512]{1,0:T(8,128)S(1)} all-reduce(f32[24,512]{1,0:T(8,128)} %fusion.61), channel_id=1, replica_groups=mesh['blade'=1,'prow'=4,'pcol'=8] {'pcol'}, use_global_device_ids=true, to_apply=%region_2.0 | all-reduce | flops 12288 | bytes 98304 | tf_op jit(solution)/shard_map/psum | solution.py:94
  117.8 17.3 %psum.115 = f32[24,1,256]{2,0,1:T(8,128)S(1)} all-reduce(f32[24,1,256]{2,0,1:T(8,128)S(1)} %convolution_bitcast_fusion.4), channel_id=1, replica_groups=mesh['blade'=1,'prow'=4,'pcol'=8] {'prow'}, use_global_device_ids=true, to_apply=%region_3.0 | all-reduce | flops 6144 | bytes 49152 | tf_op jit(solution)/shard_map/psum | solution.py:98
  135.9 4.6 copy.29
  140.5 1.1 fusion.64
  141.6 28.3 %psum.116 = f32[24,512]{1,0:T(8,128)S(1)} all-reduce(f32[24,512]{1,0:T(8,128)S(1)} %fusion.64), channel_id=1, replica_groups=mesh['blade'=1,'prow'=4,'pcol'=8] {'pcol'}, use_global_device_ids=true, to_apply=%region_4.0 | all-reduce | flops 12288 | bytes 98304 | tf_op jit(solution)/shard_map/psum | solution.py:94
  170.7 1.6 fusion.92
  172.3 17.4 %psum.117 = f32[24,256]{1,0:T(8,128)S(1)} all-reduce(f32[24,256]{1,0:T(8,128)S(1)} %fusion.92), channel_id=1, replica_groups=mesh['blade'=1,'prow'=4,'pcol'=8] {'prow'}, use_global_device_ids=true, to_apply=%region_5.0 | all-reduce | flops 6144 | bytes 49152 | tf_op jit(solution)/shard_map/psum | solution.py:98
  189.7 4.6 copy.30
  194.2 1.7 fusion.67
  196.0 27.0 %psum.118 = f32[24,512]{1,0:T(8,128)S(1)} all-reduce(f32[24,512]{1,0:T(8,128)} %fusion.67), channel_id=1, replica_groups=mesh['blade'=1,'prow'=4,'pcol'=8] {'pcol'}, use_global_device_ids=true, to_apply=%region_6.0 | all-reduce | flops 12288 | bytes 98304 | tf_op jit(solution)/shard_map/psum | solution.py:94
  223.0 20.1 %fusion.124 = (f32[4,512,1,256]{3,2,1,0:T(1,128)S(1)}, f32[4,512,1,256]{3,2,1,0:T(1,128)}, f32[4,512,1,256]{3,2,1,0:T(1,128)}, f32[4,512,1,256]{3,2,1,0:T(1,128)S(1)}) fusion(f32[4,512,4,256]{3,2,1,0:T(4,128)} %bitcast.165), kind=kLoop, calls=%fused_computation.164 | loop fusion | bytes 16777216 | tf_op jit(solution)/shard_map/slice | solution.py:102
  243.1 0.9 fusion.73
  244.7 17.4 %all-reduce.2 = (f32[24,256]{1,0:T(8,128)S(1)}, f32[24,256]{1,0:T(8,128)S(1)}) all-reduce(f32[24,256]{1,0:T(8,128)S(1)} %fusion.89, f32[24,256]{1,0:T(8,128)S(1)} %fusion.73), channel_id=1, replica_groups=mesh['blade'=1,'prow'=4,'pcol'=8] {'prow'}, use_global_device_ids=true, to_apply=%region_7.0 | all-reduce | flops 12288 | bytes 98304 | tf_op jit(solution)/shard_map/psum | solution.py:98
  262.1 1.4 convolution_bitcast_fusion.3
  263.5 28.2 %psum.121 = f32[24,1,512]{2,0,1:T(8,128)S(1)} all-reduce(f32[24,1,512]{2,0,1:T(8,128)S(1)} %convolution_bitcast_fusion.3), channel_id=1, replica_groups=mesh['blade'=1,'prow'=4,'pcol'=8] {'pcol'}, use_global_device_ids=true, to_apply=%region_9.0 | all-reduce | flops 12288 | bytes 98304 | tf_op jit(solution)/shard_map/psum | solution.py:109
  291.8 2.5 fusion.70
  294.3 18.0 %psum.122 = f32[24,256]{1,0:T(8,128)} all-reduce(f32[24,256]{1,0:T(8,128)S(1)} %fusion.70), channel_id=1, replica_groups=mesh['blade'=1,'prow'=4,'pcol'=8] {'prow'}, use_global_device_ids=true, to_apply=%region_10.0 | all-reduce | flops 6144 | bytes 49152 | tf_op jit(solution)/shard_map/psum | solution.py:105
  312.4 1.4 convolution_bitcast_fusion.2
  313.8 26.5 %psum.123 = f32[24,1,512]{2,0,1:T(8,128)S(1)} all-reduce(f32[24,1,512]{2,0,1:T(8,128)S(1)} %convolution_bitcast_fusion.2), channel_id=1, replica_groups=mesh['blade'=1,'prow'=4,'pcol'=8] {'pcol'}, use_global_device_ids=true, to_apply=%region_11.0 | all-reduce | flops 12288 | bytes 98304 | tf_op jit(solution)/shard_map/psum | solution.py:109
  340.3 2.5 fusion.76
  342.8 17.2 %psum.124 = f32[24,256]{1,0:T(8,128)S(1)} all-reduce(f32[24,256]{1,0:T(8,128)S(1)} %fusion.76), channel_id=1, replica_groups=mesh['blade'=1,'prow'=4,'pcol'=8] {'prow'}, use_global_device_ids=true, to_apply=%region_12.0 | all-reduce | flops 6144 | bytes 49152 | tf_op jit(solution)/shard_map/psum | solution.py:105
  360.4 28.2 %psum.125 = f32[24,1,512]{2,0,1:T(8,128)S(1)} all-reduce(f32[24,1,512]{2,0,1:T(8,128)S(1)} %convolution_bitcast_fusion.1), channel_id=1, replica_groups=mesh['blade'=1,'prow'=4,'pcol'=8] {'pcol'}, use_global_device_ids=true, to_apply=%region_13.0 | all-reduce | flops 12288 | bytes 98304 | tf_op jit(solution)/shard_map/psum | solution.py:109
  388.6 0.9 fusion.79
  389.6 17.6 %psum.126 = f32[24,256]{1,0:T(8,128)S(1)} all-reduce(f32[24,256]{1,0:T(8,128)S(1)} %fusion.79), channel_id=1, replica_groups=mesh['blade'=1,'prow'=4,'pcol'=8] {'prow'}, use_global_device_ids=true, to_apply=%region_14.0 | all-reduce | flops 6144 | bytes 49152 | tf_op jit(solution)/shard_map/psum | solution.py:105
  407.5 26.5 %psum.127 = f32[24,1,512]{2,0,1:T(8,128)S(1)} all-reduce(f32[24,1,512]{2,0,1:T(8,128)S(1)} %convolution_bitcast_fusion), channel_id=1, replica_groups=mesh['blade'=1,'prow'=4,'pcol'=8] {'pcol'}, use_global_device_ids=true, to_apply=%region_15.0 | all-reduce | flops 12288 | bytes 98304 | tf_op jit(solution)/shard_map/psum | solution.py:109
  434.0 16.0 %all_gather.3 = f32[24,4,2048]{2,0,1:T(8,128)S(1)} all-gather(f32[24,4,512]{2,0,1:T(8,128)S(1)} %constant_dynamic-update-slice_fusion.3), channel_id=1, replica_groups=mesh['blade'=1,'prow'=4,'pcol'=8] {'prow'}, dimensions={2}, use_global_device_ids=true | all-gather | bytes 983040 | tf_op jit(solution)/shard_map/all_gather | solution.py:111
  450.1 808.1 %while.20 = (s32[]{:T(128)}, f32[16,24,512]{2,1,0:T(8,128)S(1)}, f32[16,3,512]{2,0,1:T(8,128)S(1)}, f32[3,8192]{1,0:T(4,128)S(1)}, f32[24,8192]{1,0:T(8,128)S(1)}, /*index=5*/s32[]{:T(128)}, s32[]{:T(128)}, s32[]{}, s32[]{}) while((s32[]{:T(128)}, f32[16,24,512]{2,1,0:T(8,128)S(1)}, f32[16,3,512]{2,0,1:T(8,128)S(1)}, ...), condition=%wide.region_17.0_spmd, body=%wide.region_16.0_spmd.sunk | while | flops 1275068416 | bytes 1149061 | solution.py:126
  450.2 50.4 %fusion.144 = f32[16,24,512]{2,1,0:T(8,128)S(1)} fusion(f32[16,24,512]{2,1,0:T(8,128)S(1)} %get-tuple-element.271, s32[]{:T(128)} %get-tuple-element.270, f32[24,8192]{1,0:T(8,128)S(1)} %get-tuple-element.283, f32[8192]{0:T(1024)S(1)} %bitcast.168, f32[512]{0:T(512)S(1)} %bitcast.174, f32[8192]{0:T(1024)S(1)} %bitcast.169, f32[512]{0:T(512)S(1)} %bitcast.173, ...), kind=kOutput, calls=%fused_computation.29.clone.1 | convolution fusion | flops 1275068416 | bytes 940036 | tf_op jit(solution)/shard_map/while/body/eval_jaxpr/dot_general | solution.py:122
  500.7 50.4 %fusion.144 = f32[16,24,512]{2,1,0:T(8,128)S(1)} fusion(f32[16,24,512]{2,1,0:T(8,128)S(1)} %get-tuple-element.271, s32[]{:T(128)} %get-tuple-element.270, f32[24,8192]{1,0:T(8,128)S(1)} %get-tuple-element.283, f32[8192]{0:T(1024)S(1)} %bitcast.168, f32[512]{0:T(512)S(1)} %bitcast.174, f32[8192]{0:T(1024)S(1)} %bitcast.169, f32[512]{0:T(512)S(1)} %bitcast.173, ...), kind=kOutput, calls=%fused_computation.29.clone.1 | convolution fusion | flops 1275068416 | bytes 940036 | tf_op jit(solution)/shard_map/while/body/eval_jaxpr/dot_general | solution.py:122
  551.2 50.4 %fusion.144 = f32[16,24,512]{2,1,0:T(8,128)S(1)} fusion(f32[16,24,512]{2,1,0:T(8,128)S(1)} %get-tuple-element.271, s32[]{:T(128)} %get-tuple-element.270, f32[24,8192]{1,0:T(8,128)S(1)} %get-tuple-element.283, f32[8192]{0:T(1024)S(1)} %bitcast.168, f32[512]{0:T(512)S(1)} %bitcast.174, f32[8192]{0:T(1024)S(1)} %bitcast.169, f32[512]{0:T(512)S(1)} %bitcast.173, ...), kind=kOutput, calls=%fused_computation.29.clone.1 | convolution fusion | flops 1275068416 | bytes 940036 | tf_op jit(solution)/shard_map/while/body/eval_jaxpr/dot_general | solution.py:122
  601.7 50.4 %fusion.144 = f32[16,24,512]{2,1,0:T(8,128)S(1)} fusion(f32[16,24,512]{2,1,0:T(8,128)S(1)} %get-tuple-element.271, s32[]{:T(128)} %get-tuple-element.270, f32[24,8192]{1,0:T(8,128)S(1)} %get-tuple-element.283, f32[8192]{0:T(1024)S(1)} %bitcast.168, f32[512]{0:T(512)S(1)} %bitcast.174, f32[8192]{0:T(1024)S(1)} %bitcast.169, f32[512]{0:T(512)S(1)} %bitcast.173, ...), kind=kOutput, calls=%fused_computation.29.clone.1 | convolution fusion | flops 1275068416 | bytes 940036 | tf_op jit(solution)/shard_map/while/body/eval_jaxpr/dot_general | solution.py:122
  652.2 50.4 %fusion.144 = f32[16,24,512]{2,1,0:T(8,128)S(1)} fusion(f32[16,24,512]{2,1,0:T(8,128)S(1)} %get-tuple-element.271, s32[]{:T(128)} %get-tuple-element.270, f32[24,8192]{1,0:T(8,128)S(1)} %get-tuple-element.283, f32[8192]{0:T(1024)S(1)} %bitcast.168, f32[512]{0:T(512)S(1)} %bitcast.174, f32[8192]{0:T(1024)S(1)} %bitcast.169, f32[512]{0:T(512)S(1)} %bitcast.173, ...), kind=kOutput, calls=%fused_computation.29.clone.1 | convolution fusion | flops 1275068416 | bytes 940036 | tf_op jit(solution)/shard_map/while/body/eval_jaxpr/dot_general | solution.py:122
  702.7 50.4 %fusion.144 = f32[16,24,512]{2,1,0:T(8,128)S(1)} fusion(f32[16,24,512]{2,1,0:T(8,128)S(1)} %get-tuple-element.271, s32[]{:T(128)} %get-tuple-element.270, f32[24,8192]{1,0:T(8,128)S(1)} %get-tuple-element.283, f32[8192]{0:T(1024)S(1)} %bitcast.168, f32[512]{0:T(512)S(1)} %bitcast.174, f32[8192]{0:T(1024)S(1)} %bitcast.169, f32[512]{0:T(512)S(1)} %bitcast.173, ...), kind=kOutput, calls=%fused_computation.29.clone.1 | convolution fusion | flops 1275068416 | bytes 940036 | tf_op jit(solution)/shard_map/while/body/eval_jaxpr/dot_general | solution.py:122
  753.3 50.4 %fusion.144 = f32[16,24,512]{2,1,0:T(8,128)S(1)} fusion(f32[16,24,512]{2,1,0:T(8,128)S(1)} %get-tuple-element.271, s32[]{:T(128)} %get-tuple-element.270, f32[24,8192]{1,0:T(8,128)S(1)} %get-tuple-element.283, f32[8192]{0:T(1024)S(1)} %bitcast.168, f32[512]{0:T(512)S(1)} %bitcast.174, f32[8192]{0:T(1024)S(1)} %bitcast.169, f32[512]{0:T(512)S(1)} %bitcast.173, ...), kind=kOutput, calls=%fused_computation.29.clone.1 | convolution fusion | flops 1275068416 | bytes 940036 | tf_op jit(solution)/shard_map/while/body/eval_jaxpr/dot_general | solution.py:122
  803.8 50.4 %fusion.144 = f32[16,24,512]{2,1,0:T(8,128)S(1)} fusion(f32[16,24,512]{2,1,0:T(8,128)S(1)} %get-tuple-element.271, s32[]{:T(128)} %get-tuple-element.270, f32[24,8192]{1,0:T(8,128)S(1)} %get-tuple-element.283, f32[8192]{0:T(1024)S(1)} %bitcast.168, f32[512]{0:T(512)S(1)} %bitcast.174, f32[8192]{0:T(1024)S(1)} %bitcast.169, f32[512]{0:T(512)S(1)} %bitcast.173, ...), kind=kOutput, calls=%fused_computation.29.clone.1 | convolution fusion | flops 1275068416 | bytes 940036 | tf_op jit(solution)/shard_map/while/body/eval_jaxpr/dot_general | solution.py:122
  854.3 50.4 %fusion.144 = f32[16,24,512]{2,1,0:T(8,128)S(1)} fusion(f32[16,24,512]{2,1,0:T(8,128)S(1)} %get-tuple-element.271, s32[]{:T(128)} %get-tuple-element.270, f32[24,8192]{1,0:T(8,128)S(1)} %get-tuple-element.283, f32[8192]{0:T(1024)S(1)} %bitcast.168, f32[512]{0:T(512)S(1)} %bitcast.174, f32[8192]{0:T(1024)S(1)} %bitcast.169, f32[512]{0:T(512)S(1)} %bitcast.173, ...), kind=kOutput, calls=%fused_computation.29.clone.1 | convolution fusion | flops 1275068416 | bytes 940036 | tf_op jit(solution)/shard_map/while/body/eval_jaxpr/dot_general | solution.py:122
  904.8 50.4 %fusion.144 = f32[16,24,512]{2,1,0:T(8,128)S(1)} fusion(f32[16,24,512]{2,1,0:T(8,128)S(1)} %get-tuple-element.271, s32[]{:T(128)} %get-tuple-element.270, f32[24,8192]{1,0:T(8,128)S(1)} %get-tuple-element.283, f32[8192]{0:T(1024)S(1)} %bitcast.168, f32[512]{0:T(512)S(1)} %bitcast.174, f32[8192]{0:T(1024)S(1)} %bitcast.169, f32[512]{0:T(512)S(1)} %bitcast.173, ...), kind=kOutput, calls=%fused_computation.29.clone.1 | convolution fusion | flops 1275068416 | bytes 940036 | tf_op jit(solution)/shard_map/while/body/eval_jaxpr/dot_general | solution.py:122
  955.3 50.4 %fusion.144 = f32[16,24,512]{2,1,0:T(8,128)S(1)} fusion(f32[16,24,512]{2,1,0:T(8,128)S(1)} %get-tuple-element.271, s32[]{:T(128)} %get-tuple-element.270, f32[24,8192]{1,0:T(8,128)S(1)} %get-tuple-element.283, f32[8192]{0:T(1024)S(1)} %bitcast.168, f32[512]{0:T(512)S(1)} %bitcast.174, f32[8192]{0:T(1024)S(1)} %bitcast.169, f32[512]{0:T(512)S(1)} %bitcast.173, ...), kind=kOutput, calls=%fused_computation.29.clone.1 | convolution fusion | flops 1275068416 | bytes 940036 | tf_op jit(solution)/shard_map/while/body/eval_jaxpr/dot_general | solution.py:122
  1005.8 50.4 %fusion.144 = f32[16,24,512]{2,1,0:T(8,128)S(1)} fusion(f32[16,24,512]{2,1,0:T(8,128)S(1)} %get-tuple-element.271, s32[]{:T(128)} %get-tuple-element.270, f32[24,8192]{1,0:T(8,128)S(1)} %get-tuple-element.283, f32[8192]{0:T(1024)S(1)} %bitcast.168, f32[512]{0:T(512)S(1)} %bitcast.174, f32[8192]{0:T(1024)S(1)} %bitcast.169, f32[512]{0:T(512)S(1)} %bitcast.173, ...), kind=kOutput, calls=%fused_computation.29.clone.1 | convolution fusion | flops 1275068416 | bytes 940036 | tf_op jit(solution)/shard_map/while/body/eval_jaxpr/dot_general | solution.py:122
  1056.3 50.4 %fusion.144 = f32[16,24,512]{2,1,0:T(8,128)S(1)} fusion(f32[16,24,512]{2,1,0:T(8,128)S(1)} %get-tuple-element.271, s32[]{:T(128)} %get-tuple-element.270, f32[24,8192]{1,0:T(8,128)S(1)} %get-tuple-element.283, f32[8192]{0:T(1024)S(1)} %bitcast.168, f32[512]{0:T(512)S(1)} %bitcast.174, f32[8192]{0:T(1024)S(1)} %bitcast.169, f32[512]{0:T(512)S(1)} %bitcast.173, ...), kind=kOutput, calls=%fused_computation.29.clone.1 | convolution fusion | flops 1275068416 | bytes 940036 | tf_op jit(solution)/shard_map/while/body/eval_jaxpr/dot_general | solution.py:122
  1106.8 50.4 %fusion.144 = f32[16,24,512]{2,1,0:T(8,128)S(1)} fusion(f32[16,24,512]{2,1,0:T(8,128)S(1)} %get-tuple-element.271, s32[]{:T(128)} %get-tuple-element.270, f32[24,8192]{1,0:T(8,128)S(1)} %get-tuple-element.283, f32[8192]{0:T(1024)S(1)} %bitcast.168, f32[512]{0:T(512)S(1)} %bitcast.174, f32[8192]{0:T(1024)S(1)} %bitcast.169, f32[512]{0:T(512)S(1)} %bitcast.173, ...), kind=kOutput, calls=%fused_computation.29.clone.1 | convolution fusion | flops 1275068416 | bytes 940036 | tf_op jit(solution)/shard_map/while/body/eval_jaxpr/dot_general | solution.py:122
  1157.3 50.4 %fusion.144 = f32[16,24,512]{2,1,0:T(8,128)S(1)} fusion(f32[16,24,512]{2,1,0:T(8,128)S(1)} %get-tuple-element.271, s32[]{:T(128)} %get-tuple-element.270, f32[24,8192]{1,0:T(8,128)S(1)} %get-tuple-element.283, f32[8192]{0:T(1024)S(1)} %bitcast.168, f32[512]{0:T(512)S(1)} %bitcast.174, f32[8192]{0:T(1024)S(1)} %bitcast.169, f32[512]{0:T(512)S(1)} %bitcast.173, ...), kind=kOutput, calls=%fused_computation.29.clone.1 | convolution fusion | flops 1275068416 | bytes 940036 | tf_op jit(solution)/shard_map/while/body/eval_jaxpr/dot_general | solution.py:122
  1207.8 50.4 %fusion.144 = f32[16,24,512]{2,1,0:T(8,128)S(1)} fusion(f32[16,24,512]{2,1,0:T(8,128)S(1)} %get-tuple-element.271, s32[]{:T(128)} %get-tuple-element.270, f32[24,8192]{1,0:T(8,128)S(1)} %get-tuple-element.283, f32[8192]{0:T(1024)S(1)} %bitcast.168, f32[512]{0:T(512)S(1)} %bitcast.174, f32[8192]{0:T(1024)S(1)} %bitcast.169, f32[512]{0:T(512)S(1)} %bitcast.173, ...), kind=kOutput, calls=%fused_computation.29.clone.1 | convolution fusion | flops 1275068416 | bytes 940036 | tf_op jit(solution)/shard_map/while/body/eval_jaxpr/dot_general | solution.py:122
  1259.0 2.0 collective-permute-start
  1261.0 2.4 collective-permute-start.1
  1263.7 4.3 collective-permute-done.1
  1268.8 1.9 collective-permute-start.2
  1270.7 1.3 collective-permute-start.3
  1273.2 1.3 copy.20
  1274.6 1.5 collective-permute-done.3
  1276.1 1.2 pad_maximum_fusion
  1278.4 1.4 slice_subtract_fusion.1
  1279.9 1.3 fusion.83
  1281.1 0.9 fusion.107
  (89 shorter events, 11.7 us)
Async XLA Ops:
  9.9 8.8 copy-start.5
  243.1 1.0 copy-start
  389.5 60.5 %copy-start.3 = (f32[3,4,16,128]{3,2,1,0:T(8,128)S(1)}, f32[3,4,16,128]{3,2,1,0:T(8,128)}, u32[]{:S(2)}) copy-start(f32[3,4,16,128]{3,2,1,0:T(8,128)} %param.27) | copy-start | bytes 294916
  389.5 60.5 %copy-start.1 = (f32[3,8192]{1,0:T(4,128)S(1)}, f32[3,8192]{1,0:T(4,128)}, u32[]{:S(2)}) copy-start(f32[3,8192]{1,0:T(4,128)} %param.26) | copy-start | bytes 294916
  389.6 60.5 %copy-start.6 = (f32[16,24,512]{2,1,0:T(8,128)S(1)}, f32[16,24,512]{2,1,0:T(8,128)}, u32[]{:S(2)}) copy-start(f32[16,24,512]{2,1,0:T(8,128)} %custom-call.1) | copy-start | bytes 2359300
  1258.8 4.7 copy-start.4
  1258.9 9.8 copy-start.2
  1259.0 4.6 collective-permute-start
  1261.0 7.0 collective-permute-start.1
  1268.8 5.8 collective-permute-start.2
  1270.7 5.4 collective-permute-start.3
where the time goes:
time: 1280 us
  matrix products  827 us (65%)
  blocking collectives  363 us (28%)
  local copies, waits for them, and re-layouts  71.1 us (6%)
    dot_general x16, matrix products, deform(): lax.dot_general(coef_matrix, wendland(dist_sq), (((1,), (1,)), ((), ())),...  806 us
    psum x4, blocking collectives, shards(): summed = lax.psum(partial_value, 'pcol')  114 us
    psum x4, blocking collectives, shards(): solved = lax.psum(term, 'pcol')  109 us
    psum x4, blocking collectives, shards(): solved = lax.psum(term, 'prow')  70.5 us
    psum x3, blocking collectives, shards(): summed = lax.psum(partial_value, 'prow')  52.8 us
  transfers between devices with their start and end apart: 4, of which 3 were waited for; matrix products, arithmetic and copies ran while one was open for 0% of the time, Pallas kernels for 0%

commit v1 on v0

--- a/solution.py
+++ b/solution.py
@@ -6,6 +6,15 @@
 
 support_radius = 0.1
 highest = lax.Precision.HIGHEST
+
+
+def doubling_sum(x, mesh_axis):
+    count = lax.axis_size(mesh_axis)
+    total, stride = (x, 1)
+    while stride < count:
+        total = total + lax.ppermute(total, mesh_axis, [(i, i ^ stride) for i in range(count)])
+        stride = 2 * stride
+    return total
 
 
 def padded_2(cells, sides, width):
@@ -102,7 +111,7 @@
         col_blocks = local_factor[:, :, block_id]
         forward_block = forward[:, block_id]
         partial_value = jnp.einsum("jrc,wjr->wc", col_blocks, coeffs, precision=highest)
-        summed = lax.psum(partial_value, "prow")
+        summed = doubling_sum(partial_value, "prow")
         term = jnp.einsum(
             "ab,wa->wb", local_inverses[block_id], forward_block - summed, precision=highest
         )

time: 1280 us -> 1240 us (0.969)
  blocking collectives: 363 us -> 308 us
  starting transfers between devices: 7.53 us -> 37.3 us
  local copies, waits for them, and re-layouts: 71.1 us -> 43.9 us
    psum x3 -> x0, blocking collectives: 52.8 us -> none  [shards(): summed = lax.psum(partial_value, 'prow')]
    ppermute x0 -> x8, starting transfers between devices: none -> 26.2 us  [doubling_sum(): lax.ppermute(total, mesh_axis, [(i, i ^ stride) for i in range(count)])]
    slice x1 -> x0, local copies, waits for them, and re-layouts: 20.1 us -> none  [shards(): col_blocks = local_factor[:, :, block_id]]
  transfers between devices with their start and end apart: 4 -> 12, of which waited for: 3 -> 8; matrix products, arithmetic and copies ran while one was open for 0% -> 4% of each run, Pallas kernels for 0% -> 0%
where the time goes in v1:
time: 1240 us
  matrix products  826 us (67%)
  blocking collectives  308 us (25%)
  local copies, waits for them, and re-layouts  43.9 us (4%)
  starting transfers between devices  37.3 us (3%)
  waiting for transfers between devices  15.3 us (1%)
    dot_general x16, matrix products, deform(): lax.dot_general(coef_matrix, wendland(dist_sq), (((1,), (1,)), ((), ())),...  806 us
    psum x4, blocking collectives, shards(): summed = lax.psum(partial_value, 'pcol')  114 us
    psum x4, blocking collectives, shards(): solved = lax.psum(term, 'pcol')  110 us
    psum x4, blocking collectives, shards(): solved = lax.psum(term, 'prow')  68.8 us
    ppermute x8, starting transfers between devices, doubling_sum(): lax.ppermute(total, mesh_axis, [(i, i ^ stride) for i in range(count)])  26.2 us
  transfers between devices with their start and end apart: 12, of which 8 were waited for; matrix products, arithmetic and copies ran while one was open for 4% of the time, Pallas kernels for 0%

profile of v1, /device:TPU:1, one launch (start us, length us, event | category | flops | bytes accessed | tf_op | source)
XLA Modules:
  0.0 1239.0 jit_solution(10649028044424494560)
XLA Ops:
  0.6 5.2 copy.99
  6.9 7.0 fusion.112
  13.9 2.4 fusion.113
  16.3 4.6 copy.28
  20.8 1.1 fusion.50
  21.9 32.4 %psum.84 = f32[24,512]{1,0:T(8,128)S(1)} all-reduce(f32[24,512]{1,0:T(8,128)S(1)} %fusion.50), channel_id=1, replica_groups=mesh['blade'=1,'prow'=4,'pcol'=8] {'pcol'}, use_global_device_ids=true, to_apply=%region_0.0 | all-reduce | flops 12288 | bytes 98304 | tf_op jit(solution)/shard_map/psum | solution.py:103
  54.3 1.7 copy.13
  56.7 1.3 fusion.116
  58.6 16.8 %psum.85 = f32[24,1,256]{2,0,1:T(8,128)S(1)} all-reduce(f32[24,1,256]{2,0,1:T(8,128)S(1)} %convolution_bitcast_fusion.5), channel_id=1, replica_groups=mesh['blade'=1,'prow'=4,'pcol'=8] {'prow'}, use_global_device_ids=true, to_apply=%region_1.0 | all-reduce | flops 6144 | bytes 49152 | tf_op jit(solution)/shard_map/psum | solution.py:107
  75.4 4.6 copy.29
  80.0 1.1 fusion.53
  81.1 26.6 %psum.86 = f32[24,512]{1,0:T(8,128)S(1)} all-reduce(f32[24,512]{1,0:T(8,128)S(1)} %fusion.53), channel_id=1, replica_groups=mesh['blade'=1,'prow'=4,'pcol'=8] {'pcol'}, use_global_device_ids=true, to_apply=%region_2.0 | all-reduce | flops 12288 | bytes 98304 | tf_op jit(solution)/shard_map/psum | solution.py:103
  109.0 17.2 %psum.87 = f32[24,1,256]{2,0,1:T(8,128)S(1)} all-reduce(f32[24,1,256]{2,0,1:T(8,128)S(1)} %convolution_bitcast_fusion.4), channel_id=1, replica_groups=mesh['blade'=1,'prow'=4,'pcol'=8] {'prow'}, use_global_device_ids=true, to_apply=%region_3.0 | all-reduce | flops 6144 | bytes 49152 | tf_op jit(solution)/shard_map/psum | solution.py:107
  126.3 4.6 copy.30
  130.9 1.1 fusion.56
  132.0 28.2 %psum.88 = f32[24,512]{1,0:T(8,128)S(1)} all-reduce(f32[24,512]{1,0:T(8,128)S(1)} %fusion.56), channel_id=1, replica_groups=mesh['blade'=1,'prow'=4,'pcol'=8] {'pcol'}, use_global_device_ids=true, to_apply=%region_4.0 | all-reduce | flops 12288 | bytes 98304 | tf_op jit(solution)/shard_map/psum | solution.py:103
  161.1 1.6 fusion.76
  162.6 17.2 %psum.89 = f32[24,256]{1,0:T(8,128)S(1)} all-reduce(f32[24,256]{1,0:T(8,128)S(1)} %fusion.76), channel_id=1, replica_groups=mesh['blade'=1,'prow'=4,'pcol'=8] {'prow'}, use_global_device_ids=true, to_apply=%region_5.0 | all-reduce | flops 6144 | bytes 49152 | tf_op jit(solution)/shard_map/psum | solution.py:107
  179.8 4.6 copy.31
  184.4 1.1 fusion.59
  185.5 26.6 %psum.90 = f32[24,512]{1,0:T(8,128)S(1)} all-reduce(f32[24,512]{1,0:T(8,128)S(1)} %fusion.59), channel_id=1, replica_groups=mesh['blade'=1,'prow'=4,'pcol'=8] {'pcol'}, use_global_device_ids=true, to_apply=%region_6.0 | all-reduce | flops 12288 | bytes 98304 | tf_op jit(solution)/shard_map/psum | solution.py:103
  212.2 1.6 fusion.73
  215.5 17.6 %psum.91 = f32[24,256]{1,0:T(8,128)S(1)} all-reduce(f32[24,256]{1,0:T(8,128)S(1)} %fusion.73), channel_id=1, replica_groups=mesh['blade'=1,'prow'=4,'pcol'=8] {'prow'}, use_global_device_ids=true, to_apply=%region_7.0 | all-reduce | flops 6144 | bytes 49152 | tf_op jit(solution)/shard_map/psum | solution.py:107
  233.0 1.4 convolution_bitcast_fusion.3
  234.4 28.1 %psum.92 = f32[24,1,512]{2,0,1:T(8,128)S(1)} all-reduce(f32[24,1,512]{2,0,1:T(8,128)S(1)} %convolution_bitcast_fusion.3), channel_id=1, replica_groups=mesh['blade'=1,'prow'=4,'pcol'=8] {'pcol'}, use_global_device_ids=true, to_apply=%region_8.0 | all-reduce | flops 12288 | bytes 98304 | tf_op jit(solution)/shard_map/psum | solution.py:118
  262.5 2.5 fusion.62
  265.1 8.1 collective-permute-start.2
  274.1 2.6 collective-permute-done.3
  277.1 26.5 %psum.93 = f32[24,1,512]{2,0,1:T(8,128)S(1)} all-reduce(f32[24,1,512]{2,0,1:T(8,128)S(1)} %convolution_bitcast_fusion.2), channel_id=1, replica_groups=mesh['blade'=1,'prow'=4,'pcol'=8] {'pcol'}, use_global_device_ids=true, to_apply=%region_9.0 | all-reduce | flops 12288 | bytes 98304 | tf_op jit(solution)/shard_map/psum | solution.py:118
  303.7 2.5 fusion.64
  306.2 8.4 collective-permute-start.4
  315.5 2.6 collective-permute-done.5
  318.5 28.5 %psum.94 = f32[24,1,512]{2,0,1:T(8,128)S(1)} all-reduce(f32[24,1,512]{2,0,1:T(8,128)S(1)} %convolution_bitcast_fusion.1), channel_id=1, replica_groups=mesh['blade'=1,'prow'=4,'pcol'=8] {'pcol'}, use_global_device_ids=true, to_apply=%region_10.0 | all-reduce | flops 12288 | bytes 98304 | tf_op jit(solution)/shard_map/psum | solution.py:118
  347.0 2.5 fusion.65
  349.5 8.4 collective-permute-start.6
  358.9 2.6 collective-permute-done.7
  361.8 26.7 %psum.95 = f32[24,1,512]{2,0,1:T(8,128)S(1)} all-reduce(f32[24,1,512]{2,0,1:T(8,128)S(1)} %convolution_bitcast_fusion), channel_id=1, replica_groups=mesh['blade'=1,'prow'=4,'pcol'=8] {'pcol'}, use_global_device_ids=true, to_apply=%region_11.0 | all-reduce | flops 12288 | bytes 98304 | tf_op jit(solution)/shard_map/psum | solution.py:118
  388.6 15.9 %all_gather.3 = f32[24,4,2048]{2,0,1:T(8,128)S(1)} all-gather(f32[24,4,512]{2,0,1:T(8,128)S(1)} %constant_dynamic-update-slice_fusion.3), channel_id=1, replica_groups=mesh['blade'=1,'prow'=4,'pcol'=8] {'prow'}, dimensions={2}, use_global_device_ids=true | all-gather | bytes 983040 | tf_op jit(solution)/shard_map/all_gather | solution.py:120
  404.5 808.1 %while.20 = (s32[]{:T(128)}, f32[16,24,512]{2,1,0:T(8,128)S(1)}, f32[16,3,512]{2,0,1:T(8,128)S(1)}, f32[3,8192]{1,0:T(4,128)S(1)}, f32[24,8192]{1,0:T(8,128)S(1)}, /*index=5*/s32[]{:T(128)}, s32[]{:T(128)}, s32[]{}, s32[]{}) while((s32[]{:T(128)}, f32[16,24,512]{2,1,0:T(8,128)S(1)}, f32[16,3,512]{2,0,1:T(8,128)S(1)}, ...), condition=%wide.region_13.0_spmd, body=%wide.region_12.0_spmd.sunk | while | flops 1275068416 | bytes 1149069 | solution.py:135
  404.6 50.4 %fusion.131 = f32[16,24,512]{2,1,0:T(8,128)S(1)} fusion(f32[16,24,512]{2,1,0:T(8,128)S(1)} %get-tuple-element.265, s32[]{:T(128)S(6)} %copy.108, f32[24,8192]{1,0:T(8,128)S(1)} %get-tuple-element.277, f32[8192]{0:T(1024)S(1)} %bitcast.171, f32[512]{0:T(512)S(1)} %bitcast.177, f32[8192]{0:T(1024)S(1)} %bitcast.172, f32[512]{0:T(512)S(1)} %bitcast.176, ...), kind=kOutput, calls=%fused_computation.29.clone.1 | convolution fusion | flops 1275068416 | bytes 940036 | tf_op jit(solution)/shard_map/while/body/eval_jaxpr/dot_general | solution.py:131
  455.1 50.4 %fusion.131 = f32[16,24,512]{2,1,0:T(8,128)S(1)} fusion(f32[16,24,512]{2,1,0:T(8,128)S(1)} %get-tuple-element.265, s32[]{:T(128)S(6)} %copy.108, f32[24,8192]{1,0:T(8,128)S(1)} %get-tuple-element.277, f32[8192]{0:T(1024)S(1)} %bitcast.171, f32[512]{0:T(512)S(1)} %bitcast.177, f32[8192]{0:T(1024)S(1)} %bitcast.172, f32[512]{0:T(512)S(1)} %bitcast.176, ...), kind=kOutput, calls=%fused_computation.29.clone.1 | convolution fusion | flops 1275068416 | bytes 940036 | tf_op jit(solution)/shard_map/while/body/eval_jaxpr/dot_general | solution.py:131
  505.6 50.4 %fusion.131 = f32[16,24,512]{2,1,0:T(8,128)S(1)} fusion(f32[16,24,512]{2,1,0:T(8,128)S(1)} %get-tuple-element.265, s32[]{:T(128)S(6)} %copy.108, f32[24,8192]{1,0:T(8,128)S(1)} %get-tuple-element.277, f32[8192]{0:T(1024)S(1)} %bitcast.171, f32[512]{0:T(512)S(1)} %bitcast.177, f32[8192]{0:T(1024)S(1)} %bitcast.172, f32[512]{0:T(512)S(1)} %bitcast.176, ...), kind=kOutput, calls=%fused_computation.29.clone.1 | convolution fusion | flops 1275068416 | bytes 940036 | tf_op jit(solution)/shard_map/while/body/eval_jaxpr/dot_general | solution.py:131
  556.2 50.4 %fusion.131 = f32[16,24,512]{2,1,0:T(8,128)S(1)} fusion(f32[16,24,512]{2,1,0:T(8,128)S(1)} %get-tuple-element.265, s32[]{:T(128)S(6)} %copy.108, f32[24,8192]{1,0:T(8,128)S(1)} %get-tuple-element.277, f32[8192]{0:T(1024)S(1)} %bitcast.171, f32[512]{0:T(512)S(1)} %bitcast.177, f32[8192]{0:T(1024)S(1)} %bitcast.172, f32[512]{0:T(512)S(1)} %bitcast.176, ...), kind=kOutput, calls=%fused_computation.29.clone.1 | convolution fusion | flops 1275068416 | bytes 940036 | tf_op jit(solution)/shard_map/while/body/eval_jaxpr/dot_general | solution.py:131
  606.7 50.4 %fusion.131 = f32[16,24,512]{2,1,0:T(8,128)S(1)} fusion(f32[16,24,512]{2,1,0:T(8,128)S(1)} %get-tuple-element.265, s32[]{:T(128)S(6)} %copy.108, f32[24,8192]{1,0:T(8,128)S(1)} %get-tuple-element.277, f32[8192]{0:T(1024)S(1)} %bitcast.171, f32[512]{0:T(512)S(1)} %bitcast.177, f32[8192]{0:T(1024)S(1)} %bitcast.172, f32[512]{0:T(512)S(1)} %bitcast.176, ...), kind=kOutput, calls=%fused_computation.29.clone.1 | convolution fusion | flops 1275068416 | bytes 940036 | tf_op jit(solution)/shard_map/while/body/eval_jaxpr/dot_general | solution.py:131
  657.2 50.4 %fusion.131 = f32[16,24,512]{2,1,0:T(8,128)S(1)} fusion(f32[16,24,512]{2,1,0:T(8,128)S(1)} %get-tuple-element.265, s32[]{:T(128)S(6)} %copy.108, f32[24,8192]{1,0:T(8,128)S(1)} %get-tuple-element.277, f32[8192]{0:T(1024)S(1)} %bitcast.171, f32[512]{0:T(512)S(1)} %bitcast.177, f32[8192]{0:T(1024)S(1)} %bitcast.172, f32[512]{0:T(512)S(1)} %bitcast.176, ...), kind=kOutput, calls=%fused_computation.29.clone.1 | convolution fusion | flops 1275068416 | bytes 940036 | tf_op jit(solution)/shard_map/while/body/eval_jaxpr/dot_general | solution.py:131
  707.7 50.4 %fusion.131 = f32[16,24,512]{2,1,0:T(8,128)S(1)} fusion(f32[16,24,512]{2,1,0:T(8,128)S(1)} %get-tuple-element.265, s32[]{:T(128)S(6)} %copy.108, f32[24,8192]{1,0:T(8,128)S(1)} %get-tuple-element.277, f32[8192]{0:T(1024)S(1)} %bitcast.171, f32[512]{0:T(512)S(1)} %bitcast.177, f32[8192]{0:T(1024)S(1)} %bitcast.172, f32[512]{0:T(512)S(1)} %bitcast.176, ...), kind=kOutput, calls=%fused_computation.29.clone.1 | convolution fusion | flops 1275068416 | bytes 940036 | tf_op jit(solution)/shard_map/while/body/eval_jaxpr/dot_general | solution.py:131
  758.2 50.4 %fusion.131 = f32[16,24,512]{2,1,0:T(8,128)S(1)} fusion(f32[16,24,512]{2,1,0:T(8,128)S(1)} %get-tuple-element.265, s32[]{:T(128)S(6)} %copy.108, f32[24,8192]{1,0:T(8,128)S(1)} %get-tuple-element.277, f32[8192]{0:T(1024)S(1)} %bitcast.171, f32[512]{0:T(512)S(1)} %bitcast.177, f32[8192]{0:T(1024)S(1)} %bitcast.172, f32[512]{0:T(512)S(1)} %bitcast.176, ...), kind=kOutput, calls=%fused_computation.29.clone.1 | convolution fusion | flops 1275068416 | bytes 940036 | tf_op jit(solution)/shard_map/while/body/eval_jaxpr/dot_general | solution.py:131
  808.7 50.4 %fusion.131 = f32[16,24,512]{2,1,0:T(8,128)S(1)} fusion(f32[16,24,512]{2,1,0:T(8,128)S(1)} %get-tuple-element.265, s32[]{:T(128)S(6)} %copy.108, f32[24,8192]{1,0:T(8,128)S(1)} %get-tuple-element.277, f32[8192]{0:T(1024)S(1)} %bitcast.171, f32[512]{0:T(512)S(1)} %bitcast.177, f32[8192]{0:T(1024)S(1)} %bitcast.172, f32[512]{0:T(512)S(1)} %bitcast.176, ...), kind=kOutput, calls=%fused_computation.29.clone.1 | convolution fusion | flops 1275068416 | bytes 940036 | tf_op jit(solution)/shard_map/while/body/eval_jaxpr/dot_general | solution.py:131
  859.2 50.4 %fusion.131 = f32[16,24,512]{2,1,0:T(8,128)S(1)} fusion(f32[16,24,512]{2,1,0:T(8,128)S(1)} %get-tuple-element.265, s32[]{:T(128)S(6)} %copy.108, f32[24,8192]{1,0:T(8,128)S(1)} %get-tuple-element.277, f32[8192]{0:T(1024)S(1)} %bitcast.171, f32[512]{0:T(512)S(1)} %bitcast.177, f32[8192]{0:T(1024)S(1)} %bitcast.172, f32[512]{0:T(512)S(1)} %bitcast.176, ...), kind=kOutput, calls=%fused_computation.29.clone.1 | convolution fusion | flops 1275068416 | bytes 940036 | tf_op jit(solution)/shard_map/while/body/eval_jaxpr/dot_general | solution.py:131
  909.7 50.4 %fusion.131 = f32[16,24,512]{2,1,0:T(8,128)S(1)} fusion(f32[16,24,512]{2,1,0:T(8,128)S(1)} %get-tuple-element.265, s32[]{:T(128)S(6)} %copy.108, f32[24,8192]{1,0:T(8,128)S(1)} %get-tuple-element.277, f32[8192]{0:T(1024)S(1)} %bitcast.171, f32[512]{0:T(512)S(1)} %bitcast.177, f32[8192]{0:T(1024)S(1)} %bitcast.172, f32[512]{0:T(512)S(1)} %bitcast.176, ...), kind=kOutput, calls=%fused_computation.29.clone.1 | convolution fusion | flops 1275068416 | bytes 940036 | tf_op jit(solution)/shard_map/while/body/eval_jaxpr/dot_general | solution.py:131
  960.2 50.4 %fusion.131 = f32[16,24,512]{2,1,0:T(8,128)S(1)} fusion(f32[16,24,512]{2,1,0:T(8,128)S(1)} %get-tuple-element.265, s32[]{:T(128)S(6)} %copy.108, f32[24,8192]{1,0:T(8,128)S(1)} %get-tuple-element.277, f32[8192]{0:T(1024)S(1)} %bitcast.171, f32[512]{0:T(512)S(1)} %bitcast.177, f32[8192]{0:T(1024)S(1)} %bitcast.172, f32[512]{0:T(512)S(1)} %bitcast.176, ...), kind=kOutput, calls=%fused_computation.29.clone.1 | convolution fusion | flops 1275068416 | bytes 940036 | tf_op jit(solution)/shard_map/while/body/eval_jaxpr/dot_general | solution.py:131
  1010.7 50.4 %fusion.131 = f32[16,24,512]{2,1,0:T(8,128)S(1)} fusion(f32[16,24,512]{2,1,0:T(8,128)S(1)} %get-tuple-element.265, s32[]{:T(128)S(6)} %copy.108, f32[24,8192]{1,0:T(8,128)S(1)} %get-tuple-element.277, f32[8192]{0:T(1024)S(1)} %bitcast.171, f32[512]{0:T(512)S(1)} %bitcast.177, f32[8192]{0:T(1024)S(1)} %bitcast.172, f32[512]{0:T(512)S(1)} %bitcast.176, ...), kind=kOutput, calls=%fused_computation.29.clone.1 | convolution fusion | flops 1275068416 | bytes 940036 | tf_op jit(solution)/shard_map/while/body/eval_jaxpr/dot_general | solution.py:131
  1061.2 50.4 %fusion.131 = f32[16,24,512]{2,1,0:T(8,128)S(1)} fusion(f32[16,24,512]{2,1,0:T(8,128)S(1)} %get-tuple-element.265, s32[]{:T(128)S(6)} %copy.108, f32[24,8192]{1,0:T(8,128)S(1)} %get-tuple-element.277, f32[8192]{0:T(1024)S(1)} %bitcast.171, f32[512]{0:T(512)S(1)} %bitcast.177, f32[8192]{0:T(1024)S(1)} %bitcast.172, f32[512]{0:T(512)S(1)} %bitcast.176, ...), kind=kOutput, calls=%fused_computation.29.clone.1 | convolution fusion | flops 1275068416 | bytes 940036 | tf_op jit(solution)/shard_map/while/body/eval_jaxpr/dot_general | solution.py:131
  1111.8 50.4 %fusion.131 = f32[16,24,512]{2,1,0:T(8,128)S(1)} fusion(f32[16,24,512]{2,1,0:T(8,128)S(1)} %get-tuple-element.265, s32[]{:T(128)S(6)} %copy.108, f32[24,8192]{1,0:T(8,128)S(1)} %get-tuple-element.277, f32[8192]{0:T(1024)S(1)} %bitcast.171, f32[512]{0:T(512)S(1)} %bitcast.177, f32[8192]{0:T(1024)S(1)} %bitcast.172, f32[512]{0:T(512)S(1)} %bitcast.176, ...), kind=kOutput, calls=%fused_computation.29.clone.1 | convolution fusion | flops 1275068416 | bytes 940036 | tf_op jit(solution)/shard_map/while/body/eval_jaxpr/dot_general | solution.py:131
  1162.3 50.4 %fusion.131 = f32[16,24,512]{2,1,0:T(8,128)S(1)} fusion(f32[16,24,512]{2,1,0:T(8,128)S(1)} %get-tuple-element.265, s32[]{:T(128)S(6)} %copy.108, f32[24,8192]{1,0:T(8,128)S(1)} %get-tuple-element.277, f32[8192]{0:T(1024)S(1)} %bitcast.171, f32[512]{0:T(512)S(1)} %bitcast.177, f32[8192]{0:T(1024)S(1)} %bitcast.172, f32[512]{0:T(512)S(1)} %bitcast.176, ...), kind=kOutput, calls=%fused_computation.29.clone.1 | convolution fusion | flops 1275068416 | bytes 940036 | tf_op jit(solution)/shard_map/while/body/eval_jaxpr/dot_general | solution.py:131
  1213.4 3.3 collective-permute-start.8
  1216.8 1.9 collective-permute-start.9
  1219.5 4.3 collective-permute-done.9
  1224.6 1.3 collective-permute-start.11
  1225.9 4.6 collective-permute-start.10
  1231.7 1.3 copy.22
  1233.1 1.2 pad_maximum_fusion
  1235.4 1.4 slice_subtract_fusion.1
  1236.9 1.3 fusion.67
  (109 shorter events, 17.2 us)
Async XLA Ops:
  0.6 6.3 copy-start.1
  5.8 8.1 copy-start
  6.7 7.1 copy-start.3
  6.8 207.0 %collective-permute-start = (f32[24,256]{1,0:T(8,128)S(1)}, f32[24,256]{1,0:T(8,128)}, u32[]{:S(2)}, u32[]{:S(2)}) collective-permute-start(f32[24,256]{1,0:T(8,128)S(1)} %fusion.63), channel_id=1, source_target_pairs={{0,8},{8,0},{16,24},{24,16},{1,9},{9,1},{17,25},{25,17},{2,10},{10... | collective-permute-start | bytes 73736 | tf_op jit(solution)/shard_map/ppermute | solution.py:15
  185.5 91.2 %copy-start.2 = (f32[1,1,256,1,512]{4,3,2,1,0:T(1,128)S(1)}, f32[1,1,256,1,512]{4,3,2,1,0:T(1,128)}, u32[]{:S(2)}) copy-start(f32[1,1,256,1,512]{4,3,2,1,0:T(1,128)} %get-tuple-element.193) | copy-start | bytes 1572868
  214.5 18.5 %collective-permute-start.1 = (f32[24,256]{1,0:T(8,128)S(1)}, f32[24,256]{1,0:T(8,128)S(1)}, u32[]{:S(2)}, u32[]{:S(2)}) collective-permute-start(f32[24,256]{1,0:T(8,128)S(1)} %add.116), channel_id=1, source_target_pairs={{0,16},{8,24},{16,0},{24,8},{1,17},{9,25},{17,1},{25,9},{2,18},{10... | collective-permute-start | bytes 73736 | tf_op jit(solution)/shard_map/ppermute | solution.py:15
  265.1 9.0 collective-permute-start.2
  274.0 2.7 collective-permute-start.3
  306.2 52.7 %copy-start.6 = (f32[3,4,16,128]{3,2,1,0:T(8,128)S(1)}, f32[3,4,16,128]{3,2,1,0:T(8,128)}, u32[]{:S(2)}) copy-start(f32[3,4,16,128]{3,2,1,0:T(8,128)} %param.27) | copy-start | bytes 294916
  306.2 9.2 collective-permute-start.4
  315.4 2.7 collective-permute-start.5
  349.5 55.0 %copy-start.4 = (f32[3,8192]{1,0:T(4,128)S(1)}, f32[3,8192]{1,0:T(4,128)}, u32[]{:S(2)}) copy-start(f32[3,8192]{1,0:T(4,128)} %param.26) | copy-start | bytes 294916
  349.5 9.2 collective-permute-start.6
  358.8 2.7 collective-permute-start.7
  361.8 42.7 %copy-start.8 = (f32[16,24,512]{2,1,0:T(8,128)S(1)}, f32[16,24,512]{2,1,0:T(8,128)}, u32[]{:S(2)}) copy-start(f32[16,24,512]{2,1,0:T(8,128)} %custom-call.1) | copy-start | bytes 2359300
  1213.3 6.1 copy-start.7
  1213.4 11.2 copy-start.5
  1213.4 5.9 collective-permute-start.8
  1216.8 7.0 collective-permute-start.9
  1224.6 8.5 collective-permute-start.11
  1225.9 7.2 collective-permute-start.10
